TPU v7x, 512 devices: a whole 4x8x8 slice. The times are simulated.
512 devices in a mesh: grid: 16 (over y, core), tile: 32 (over x, z).
Axes of the slice: x: 4, y: 8, z: 8, core: 2. Of those that a mesh axis runs over, the one named last changes fastest.
Arguments:
- rhs_local: bfloat16 [192, 786432], P(None, ('grid', 'tile')), may hold values from -6 to 6
- diag_inv: bfloat16 [1536, 512, 512], P(('grid', 'tile')), may hold values from -1 to 2, as said below
- codes: bfloat16 [327680, 1536], P(('grid', 'tile')), may hold values from -127 to 127, as said below
- row_scales: float32 [327680], P(('grid', 'tile')), may hold values from 0 to 1, as said below
- sep_index: int32 [327680], P(('grid', 'tile')), may hold values from 0 to 2559, as said below
- live_rows: int32 [512], P(('grid', 'tile')), may hold values from 160 to 640, as said below
- rhs_sep: bfloat16 [192, 2560], P(None, 'tile'), may hold values from -6 to 6
- root_inv: bfloat16 [2560, 2560], P('tile'), may hold values from -1 to 2, as said below
Outputs:
- solution_local: bfloat16 [192, 786432], P(None, ('grid', 'tile'))
- solution_sep: float32 [192, 2560], P(None, 'tile')
Inputs may be any that keep to these rules, and one draw needn't show every extreme that they name: `diag_inv`: each block is upper triangular. `root_inv`: each block is upper triangular. `codes`: Integers. `row_scales`: Positive. `sep_index`: of each device's 640 entries, the j-th run of 20 consecutive entries lies in j * 80 to (j + 1) * 80 - 1, and the entries of one run are distinct. `live_rows`: some device has all 640 rows live.
All inputs are finite; a program needn't handle non-finite values.
Results may differ from a plain program's by a relative error of at most 0.0054.
Values may be sent and summed in bfloat16 or wider, within the bound.
No kernel may reach another device: no remote copies, remote signals or barrier semaphores. Data moves between devices by JAX's collectives and lax.ppermute only.
A program may use at most 64 MiB of HBM per device.

v0:
```python
import jax
import jax.numpy as jnp
from jax import lax
from jax.sharding import PartitionSpec as P


def selector(offsets, share_len):
    columns = jnp.arange(share_len, dtype=jnp.int32)
    return (offsets[:, :, None] == columns[None, None, :]).astype(jnp.float32)


def on_device(rhs_local, diag_inv, codes, row_scales, sep_index, live_rows, rhs_sep, root_inv):
    rhs_count, local_len = rhs_local.shape
    per_dev, block_len = (diag_inv.shape[0], diag_inv.shape[1])
    coupled_rows = codes.shape[0]
    share_len, sep_len = root_inv.shape
    tile_count = lax.axis_size("tile")
    per_share = coupled_rows // tile_count
    pieces = []
    for block_pos in range(per_dev):
        columns = rhs_local[:, block_pos * block_len : (block_pos + 1) * block_len]
        pieces.append(jnp.dot(columns, diag_inv[block_pos], preferred_element_type=jnp.float32))
    forward_flat = jnp.concatenate(pieces, axis=1).astype(jnp.bfloat16)
    positions = jnp.arange(coupled_rows, dtype=jnp.int32)
    row_factor = row_scales * (positions < live_rows[0]).astype(jnp.float32)
    coupled = (
        lax.dot_general(
            forward_flat, codes, (((1,), (1,)), ((), ())), preferred_element_type=jnp.float32
        )
        * row_factor[None, :]
    )
    bases = (jnp.arange(tile_count, dtype=jnp.int32) * share_len)[:, None]
    local_offsets = sep_index.reshape(tile_count, per_share) - bases
    onehot = selector(local_offsets, share_len)
    values = coupled.reshape(rhs_count, tile_count, per_share)
    partial_value = jnp.einsum(
        "rjp,jps->rjs", values, onehot, precision=lax.Precision.HIGHEST
    ).reshape(rhs_count, sep_len)
    summed = lax.psum(partial_value, ("grid", "tile"))
    own_share = lax.dynamic_slice_in_dim(summed, lax.axis_index("tile") * share_len, share_len, 1)
    residue = (rhs_sep.astype(jnp.float32) - own_share).astype(jnp.bfloat16)
    root_part = jnp.dot(residue, root_inv, preferred_element_type=jnp.float32)
    forward_sep = lax.psum(root_part, "tile").astype(jnp.bfloat16)
    solved = lax.dot_general(
        forward_sep, root_inv, (((1,), (1,)), ((), ())), preferred_element_type=jnp.float32
    )
    gathered = lax.all_gather(solved.astype(jnp.bfloat16), "tile", axis=1, tiled=True)
    gathered_split = gathered.astype(jnp.float32).reshape(rhs_count, tile_count, share_len)
    picked = jnp.einsum(
        "rjs,jps->rjp", gathered_split, onehot, precision=lax.Precision.HIGHEST
    ).reshape(rhs_count, coupled_rows)
    weighted = (picked * row_factor[None, :]).astype(jnp.bfloat16)
    update = jnp.dot(weighted, codes, preferred_element_type=jnp.float32)
    misfit = (forward_flat.astype(jnp.float32) - update).astype(jnp.bfloat16)
    results = []
    for block_pos in range(per_dev):
        columns = misfit[:, block_pos * block_len : (block_pos + 1) * block_len]
        results.append(
            lax.dot_general(
                columns,
                diag_inv[block_pos],
                (((1,), (1,)), ((), ())),
                preferred_element_type=jnp.float32,
            )
        )
    result = jnp.concatenate(results, axis=1)
    return (result.astype(jnp.bfloat16), solved)


def solution(mesh):
    return jax.shard_map(
        on_device,
        mesh=mesh,
        in_specs=(
            P(None, ("grid", "tile")),
            P(("grid", "tile"), None, None),
            P(("grid", "tile"), None),
            P(("grid", "tile")),
            P(("grid", "tile")),
            P(("grid", "tile")),
            P(None, "tile"),
            P("tile", None),
        ),
        out_specs=(P(None, ("grid", "tile")), P(None, "tile")),
        check_vma=False,
    )
```

profile of v0, /device:TPU:34, one launch (start us, length us, event | category | flops | bytes accessed | tf_op | source)
XLA Modules:
  0.0 530.7 jit_solution(14506760942146203309)
XLA Ops:
  7.2 0.0 all-reduce.3.cloned.1.call-start
  7.2 1.5 convolution_convert_fusion.3
  8.8 1.5 convolution_convert_fusion.4
  10.3 1.5 convolution_convert_fusion.5
  12.5 0.8 convolution_multiply_fusion
  13.3 0.2 copy.12
  13.6 0.1 reshape.44
  13.6 0.4 copy-done.3
  14.0 0.1 reshape.43
  14.1 0.1 broadcast_subtract_fusion
  14.2 3.0 fusion.15
  17.2 285.0 %all-reduce.3.cloned.1.call-done = f32[192,2560]{0,1:T(8,128)} async-done(((f32[192,2560]{0,1:T(8,128)}), f32[192,2560]{0,1:T(8,128)}) %all-reduce.3.cloned.1.call-update) | async-done | bytes 1966096 | tf_op jit(solution)/shard_map/psum | solution.py:39
  302.2 2.6 fusion.25
  304.8 154.0 %all-reduce.4 = bf16[192,2560]{1,0:T(8,128)(2,1)S(1)} all-reduce(f32[192,2560]{1,0:T(8,128)} %fusion.25), channel_id=1, replica_groups=mesh['grid'=16,'tile'=32] {'tile'}, use_global_device_ids=true, to_apply=%region_1.0 | all-reduce | flops 491520 | bytes 2949120 | tf_op jit(solution)/shard_map/psum | solution.py:43
  458.8 1.1 fusion.29
  459.8 59.6 %all_gather.3 = bf16[192,2560]{0,1:T(8,128)(2,1)S(1)} all-gather(bf16[192,80]{0,1:T(8,128)(2,1)S(1)} %get-tuple-element.2), channel_id=1, replica_groups=mesh['grid'=16,'tile'=32] {'tile'}, dimensions={1}, use_global_device_ids=true | all-gather | bytes 1013760 | tf_op jit(solution)/shard_map/all_gather | solution.py:47
  519.5 0.4 convolution_bitcast_fusion
  519.8 0.1 reshape.47
  519.9 0.2 copy.13
  520.1 1.9 fusion
  522.0 0.3 convolution_convert_fusion
  522.4 0.3 convolution_convert_fusion.1
  522.7 0.3 convolution_convert_fusion.2
  523.0 0.9 pad_maximum_fusion.1
  (20 shorter events, 0.1 us)
Async XLA Ops:
  7.2 5.3 %copy-start = (bf16[640,1536]{1,0:T(8,128)(2,1)S(1)}, bf16[640,1536]{1,0:T(8,128)(2,1)}, u32[]{:S(2)}) copy-start(bf16[640,1536]{1,0:T(8,128)(2,1)} %param.10) | copy-start | bytes 5898244
  7.2 5.3 copy-start.4
  7.2 295.0 %all-reduce.3.cloned.1.call-start = ((), (), s32[]{:S(2)}) async-start(), calls=%async_computation | async-start | bytes 5242880 | tf_op jit(solution)/shard_map/psum | solution.py:39
  8.8 3.7 copy-start.6
  10.3 2.2 copy-start.7
  11.8 0.7 copy-start.8
  13.3 0.7 copy-start.3
  17.1 285.0 %copy-start.1 = (bf16[80,2560]{1,0:T(8,128)(2,1)S(1)}, bf16[80,2560]{1,0:T(8,128)(2,1)}, u32[]{:S(2)}) copy-start(bf16[80,2560]{1,0:T(8,128)(2,1)} %param.15) | copy-start | bytes 1228804
  17.1 285.0 %copy-start.2 = (bf16[192,80]{0,1:T(8,128)(2,1)S(1)}, bf16[192,80]{0,1:T(8,128)(2,1)}, u32[]{:S(2)}) copy-start(bf16[192,80]{0,1:T(8,128)(2,1)} %param.14) | copy-start | bytes 92164
  520.1 1.9 copy-start.5
Sparse Core Ops, SparseCore 0:
  17.3 284.8 all-reduce.2
where the time goes:
time: 531 us
  waiting for transfers between devices  285 us (54%)
  blocking collectives  214 us (40%)
  matrix products  15.1 us (3%)
  between operations  14.9 us (3%)
    psum x1, waiting for transfers between devices, on_device(): summed = lax.psum(partial_value, ('grid', 'tile'))  285 us
    psum x1, blocking collectives, on_device(): forward_sep = lax.psum(root_part, 'tile').astype(jnp.bfloat16)  154 us
    all_gather x1, blocking collectives, on_device(): lax.all_gather(solved.astype(jnp.bfloat16), 'tile', axis=1, tiled=True)  59.6 us
  transfers between devices with their start and end apart: 1, of which 1 were waited for; matrix products, arithmetic and copies ran while one was open for 0% of the time, Pallas kernels for 0%

commit v1 on v0

--- a/solution.py
+++ b/solution.py
@@ -36,7 +36,9 @@
     partial_value = jnp.einsum(
         "rjp,jps->rjs", values, onehot, precision=lax.Precision.HIGHEST
     ).reshape(rhs_count, sep_len)
-    summed = lax.psum(partial_value, ("grid", "tile"))
+    summed = partial_value
+    for over in ("grid", "tile"):
+        summed = lax.psum(summed, over)
     own_share = lax.dynamic_slice_in_dim(summed, lax.axis_index("tile") * share_len, share_len, 1)
     residue = (rhs_sep.astype(jnp.float32) - own_share).astype(jnp.bfloat16)
     root_part = jnp.dot(residue, root_inv, preferred_element_type=jnp.float32)

time: 531 us -> 544 us (1.024)
  the two profiles are of different devices: /device:TPU:34 before, /device:TPU:10 now
where the time goes in v1:
time: 544 us; the launch traced here: 543 us
  waiting for transfers between devices  298 us (55%)
  blocking collectives  214 us (39%)
  matrix products  15.2 us (3%)
  between operations  15 us (3%)
    psum x2, waiting for transfers between devices, on_device(): summed = lax.psum(summed, over)  298 us
    psum x1, blocking collectives, on_device(): forward_sep = lax.psum(root_part, 'tile').astype(jnp.bfloat16)  154 us
    all_gather x1, blocking collectives, on_device(): lax.all_gather(solved.astype(jnp.bfloat16), 'tile', axis=1, tiled=True)  59.8 us
  transfers between devices with their start and end apart: 2, of which 2 were waited for; matrix products, arithmetic and copies ran while one was open for 0% of the time, Pallas kernels for 0%

profile of v1, /device:TPU:10, one launch (start us, length us, event | category | flops | bytes accessed | tf_op | source)
XLA Modules:
  0.0 543.4 jit_solution(18255381456391957552)
XLA Ops:
  7.2 1.5 convolution_convert_fusion.3
  8.8 1.5 convolution_convert_fusion.4
  10.3 1.5 convolution_convert_fusion.5
  12.5 0.8 convolution_multiply_fusion
  13.3 0.2 copy.12
  13.6 0.1 reshape.44
  13.6 0.4 copy-done.3
  14.0 0.1 reshape.43
  14.1 0.1 broadcast_subtract_fusion
  14.2 3.0 fusion.15
  17.2 123.9 %all-reduce.4.cloned.1.call-done = f32[192,2560]{0,1:T(8,128)} async-done(((f32[192,2560]{0,1:T(8,128)}), f32[192,2560]{0,1:T(8,128)}) %all-reduce.4.cloned.1.call-update) | async-done | bytes 1966096 | tf_op jit(solution)/shard_map/psum | solution.py:41
  141.2 173.8 %all-reduce.6.cloned.1.call-done = f32[192,2560]{0,1:T(8,128)} async-done(((f32[192,2560]{0,1:T(8,128)}), f32[192,2560]{0,1:T(8,128)}) %all-reduce.6.cloned.1.call-update) | async-done | bytes 1966096 | tf_op jit(solution)/shard_map/psum | solution.py:41
  314.9 2.6 fusion.25
  317.6 153.7 %all-reduce.7 = bf16[192,2560]{1,0:T(8,128)(2,1)S(1)} all-reduce(f32[192,2560]{1,0:T(8,128)} %fusion.25), channel_id=1, replica_groups=mesh['grid'=16,'tile'=32] {'tile'}, use_global_device_ids=true, to_apply=%region_2.0 | all-reduce | flops 491520 | bytes 2949120 | tf_op jit(solution)/shard_map/psum | solution.py:45
  471.3 1.1 fusion.29
  472.4 59.8 %all_gather.3 = bf16[192,2560]{0,1:T(8,128)(2,1)S(1)} all-gather(bf16[192,80]{0,1:T(8,128)(2,1)S(1)} %get-tuple-element.2), channel_id=1, replica_groups=mesh['grid'=16,'tile'=32] {'tile'}, dimensions={1}, use_global_device_ids=true | all-gather | bytes 1013760 | tf_op jit(solution)/shard_map/all_gather | solution.py:49
  532.2 0.4 convolution_bitcast_fusion
  532.5 0.1 reshape.47
  532.6 0.2 copy.13
  532.9 1.9 fusion
  534.7 0.3 convolution_convert_fusion
  535.1 0.3 convolution_convert_fusion.1
  535.4 0.3 convolution_convert_fusion.2
  535.7 0.9 pad_maximum_fusion.1
  (23 shorter events, 0.2 us)
Async XLA Ops:
  7.2 5.3 copy-start
  7.2 5.3 copy-start.4
  7.2 133.9 %all-reduce.4.cloned.1.call-start = ((), (), s32[]{:S(2)}) async-start(), calls=%async_computation | async-start | bytes 5242880 | tf_op jit(solution)/shard_map/psum | solution.py:41
  8.8 3.7 copy-start.6
  10.3 2.2 copy-start.7
  11.8 0.7 copy-start.8
  13.3 0.7 copy-start.3
  17.2 297.8 %copy-start.1 = (bf16[80,2560]{1,0:T(8,128)(2,1)S(1)}, bf16[80,2560]{1,0:T(8,128)(2,1)}, u32[]{:S(2)}) copy-start(bf16[80,2560]{1,0:T(8,128)(2,1)} %param.15) | copy-start | bytes 1228804
  17.2 297.7 %copy-start.2 = (bf16[192,80]{0,1:T(8,128)(2,1)S(1)}, bf16[192,80]{0,1:T(8,128)(2,1)}, u32[]{:S(2)}) copy-start(bf16[192,80]{0,1:T(8,128)(2,1)} %param.14) | copy-start | bytes 92164
  17.2 297.7 %all-reduce.6.cloned.1.call-start = ((), (), s32[]{:S(2)}) async-start(), calls=%async_computation.1 | async-start | bytes 5242880 | tf_op jit(solution)/shard_map/psum | solution.py:41
  532.8 1.9 copy-start.5
Sparse Core Ops, SparseCore 0:
  17.3 123.8 all-reduce.3
  144.7 170.1 all-reduce.5

commit v2 on v0

--- a/solution.py
+++ b/solution.py
@@ -44,7 +44,11 @@
     solved = lax.dot_general(
         forward_sep, root_inv, (((1,), (1,)), ((), ())), preferred_element_type=jnp.float32
     )
-    gathered = lax.all_gather(solved.astype(jnp.bfloat16), "tile", axis=1, tiled=True)
+    part = solved.astype(jnp.bfloat16)
+    count = lax.axis_size("tile")
+    shards = jnp.stack([part for _ in range(count)])
+    shards = lax.all_to_all(shards, "tile", split_axis=0, concat_axis=0)
+    gathered = jnp.concatenate(shards, axis=1)
     gathered_split = gathered.astype(jnp.float32).reshape(rhs_count, tile_count, share_len)
     picked = jnp.einsum(
         "rjs,jps->rjp", gathered_split, onehot, precision=lax.Precision.HIGHEST

time: 531 us -> 515 us (0.970)
  the two profiles are of different devices: /device:TPU:34 before, /device:TPU:64 now
where the time goes in v2:
time: 515 us; the launch traced here: 514 us
  waiting for transfers between devices  285 us (55%)
  blocking collectives  198 us (38%)
  matrix products  15.1 us (3%)
  between operations  14.9 us (3%)
    psum x1, waiting for transfers between devices, on_device(): summed = lax.psum(partial_value, ('grid', 'tile'))  285 us
    psum x1, blocking collectives, on_device(): forward_sep = lax.psum(root_part, 'tile').astype(jnp.bfloat16)  167 us
    all_to_all x1, blocking collectives, on_device(): shards = lax.all_to_all(shards, 'tile', split_axis=0, concat_axis=0)  30.5 us
  transfers between devices with their start and end apart: 1, of which 1 were waited for; matrix products, arithmetic and copies ran while one was open for 0% of the time, Pallas kernels for 0%

profile of v2, /device:TPU:64, one launch (start us, length us, event | category | flops | bytes accessed | tf_op | source)
XLA Modules:
  0.0 514.4 jit_solution(1600668212604616154)
XLA Ops:
  7.2 1.5 convolution_convert_fusion.3
  8.8 1.5 convolution_convert_fusion.4
  10.3 1.5 convolution_convert_fusion.5
  12.5 0.8 convolution_multiply_fusion
  13.3 0.2 copy.12
  13.6 0.1 reshape.49
  13.6 0.4 copy-done.3
  14.0 0.1 reshape.48
  14.1 0.1 broadcast_subtract_fusion
  14.2 3.0 fusion.20
  17.2 284.6 %all-reduce.3.cloned.1.call-done = f32[192,2560]{0,1:T(8,128)} async-done(((f32[192,2560]{0,1:T(8,128)}), f32[192,2560]{0,1:T(8,128)}) %all-reduce.3.cloned.1.call-update) | async-done | bytes 1966096 | tf_op jit(solution)/shard_map/psum | solution.py:39
  301.7 2.6 fusion.30
  304.3 167.2 %all-reduce.4 = bf16[192,2560]{1,0:T(8,128)(2,1)S(1)} all-reduce(f32[192,2560]{1,0:T(8,128)} %fusion.30), channel_id=1, replica_groups=mesh['grid'=16,'tile'=32] {'tile'}, use_global_device_ids=true, to_apply=%region_1.0 | all-reduce | flops 491520 | bytes 2949120 | tf_op jit(solution)/shard_map/psum | solution.py:43
  471.6 1.1 fusion.34
  472.6 0.1 stack.2
  472.7 30.5 %all_to_all.5 = bf16[32,192,80]{1,2,0:T(8,128)(2,1)S(1)} all-to-all(bf16[32,192,80]{1,2,0:T(8,128)(2,1)S(1)} %stack.2), channel_id=1, replica_groups=mesh['grid'=16,'tile'=32] {'tile'}, dimensions={0} | all-to-all | bytes 1966080 | tf_op jit(solution)/shard_map/all_to_all | solution.py:50
  503.2 0.4 fusion.3
  503.5 0.1 reshape.52
  503.6 0.2 copy.13
  503.9 1.9 fusion
  505.8 0.3 convolution_convert_fusion
  506.1 0.3 convolution_convert_fusion.1
  506.4 0.3 convolution_convert_fusion.2
  506.7 0.9 pad_maximum_fusion.1
  (21 shorter events, 0.1 us)
Async XLA Ops:
  7.2 5.3 %copy-start = (bf16[640,1536]{1,0:T(8,128)(2,1)S(1)}, bf16[640,1536]{1,0:T(8,128)(2,1)}, u32[]{:S(2)}) copy-start(bf16[640,1536]{1,0:T(8,128)(2,1)} %param.10) | copy-start | bytes 5898244
  7.2 5.3 %copy-start.4 = (f32[640]{0:T(1024)S(1)}, f32[640]{0:T(1024)}, u32[]{:S(2)}) copy-start(f32[640]{0:T(1024)} %param.11) | copy-start | bytes 7684
  7.2 294.5 %all-reduce.3.cloned.1.call-start = ((), (), s32[]{:S(2)}) async-start(), calls=%async_computation.1 | async-start | bytes 5242880 | tf_op jit(solution)/shard_map/psum | solution.py:39
  8.8 3.7 copy-start.6
  10.3 2.2 copy-start.7
  11.8 0.7 copy-start.8
  13.3 0.7 copy-start.3
  17.1 284.6 %copy-start.1 = (bf16[80,2560]{1,0:T(8,128)(2,1)S(1)}, bf16[80,2560]{1,0:T(8,128)(2,1)}, u32[]{:S(2)}) copy-start(bf16[80,2560]{1,0:T(8,128)(2,1)} %param.15) | copy-start | bytes 1228804
  17.1 284.6 %copy-start.2 = (bf16[192,80]{0,1:T(8,128)(2,1)S(1)}, bf16[192,80]{0,1:T(8,128)(2,1)}, u32[]{:S(2)}) copy-start(bf16[192,80]{0,1:T(8,128)(2,1)} %param.14) | copy-start | bytes 92164
  503.8 1.9 copy-start.5
Sparse Core Ops, SparseCore 0:
  17.3 284.3 all-reduce.2
